TPU v7x, 512 devices: a whole 4x8x8 slice. The times are simulated.
512 devices in a mesh: cuts: 4 (over y_hi, core), mode: 128 (over x, y_lo, z).
Axes of the slice: x: 4, y: 8 (y_hi: 2, y_lo: 4; y = y_hi * 4 + y_lo), z: 8, core: 2. Of those that a mesh axis runs over, the one named last changes fastest.
Arguments:
- stem: bfloat16 [4, 2, 1024, 16384], P('cuts', None, None, 'mode'), may hold values from -6 to 6
- branches: bfloat16 [3, 2, 1024, 1024], P(None, None, None, 'mode'), may hold values from -0.125 to 0.125
- order: int32 [3], replicated, may hold values from 0 to 2, each once
- swap_order: int32 [3, 1024], replicated, may hold values from 0 to 1023, each once within a row
- row_bits: int32 [2048], replicated, may hold values from 0 to 1023
- column_bits: int32 [2048], replicated, may hold values from 0 to 16383
Outputs:
- stem_out: bfloat16 [4, 2, 1024, 16384], P('cuts', None, None, 'mode')
- amplitudes: float32 [2, 2048], P(None, ('cuts', 'mode'))
All inputs are finite; a program needn't handle non-finite values.
Results may differ from a plain program's by a relative error of at most 0.009.
Values may be sent and summed in bfloat16 or wider, within the bound.
A program may use at most 128 MiB of HBM per device.

v0:
```python
import jax
import jax.numpy as jnp
from jax import lax
from jax.sharding import Mesh
from jax.sharding import PartitionSpec as P

MODE = ("mode_0", "mode_1", "mode_2")
CUTS_MODE = ("cuts_0", "cuts_1", "mode_0", "mode_1", "mode_2")
CUTS = ("cuts_0", "cuts_1")


def cut_rows(length, count):
    unit = 8 if length >= 8 * count else 1
    return [length // unit * k // count * unit for k in range(1, count)]


def gather_in_order(shard, axes, turns):
    blocks = shard[None]
    for k in turns:
        blocks = lax.all_gather(blocks, axes[k], axis=0, tiled=True)
    held = [lax.axis_size(axes[k]) for k in reversed(turns)]
    blocks = blocks.reshape(*held, *shard.shape)
    turned = sorted(range(len(turns)), key=lambda place: turns[len(turns) - 1 - place])
    return blocks.transpose(*turned, *range(len(turns), blocks.ndim)).reshape(-1, *shard.shape)


def joined_along(blocks, dim):
    blocks = jnp.moveaxis(blocks, 0, dim)
    dims = blocks.shape
    return blocks.reshape(*dims[:dim], dims[dim] * dims[dim + 1], *dims[dim + 2 :])


def gather_at_once(shard, axes, dim):
    cut = max(range(max(1, shard.ndim - 1)), key=lambda d: shard.shape[d])
    count, finished = (len(axes), [])
    for initial, slab in enumerate(jnp.split(shard, cut_rows(shard.shape[cut], count), axis=cut)):
        if slab.size:
            turns = [(initial - k) % count for k in range(count)]
            finished.append(gather_in_order(slab, axes, turns))
    return joined_along(jnp.concatenate(finished, axis=cut + 1), dim)


def over_axes(shard, axes):
    for axis in axes:
        shard = lax.psum(shard, axis)
    return shard


def absorb(matrix, part):
    numbers = (((0,), (0,)), ((), ()))

    def product(left, right):
        return lax.dot_general(left, right, numbers, preferred_element_type=jnp.float32)

    real = product(matrix[0], part[0]) - product(matrix[1], part[1])
    imag = product(matrix[0], part[1]) + product(matrix[1], part[0])
    return jnp.stack([real, imag], axis=0)


def body(stem, branches, order, swap_order, row_bits, column_bits):
    local = stem[0]
    groups = lax.axis_size(MODE)
    width = local.shape[1]
    rows = local.shape[2]
    everything = gather_at_once(branches, MODE, 3)
    for step in range(swap_order.shape[0]):
        moved = jnp.take(local, swap_order[step], axis=1)
        view = moved.reshape(2, groups, width // groups, rows)
        swapped = lax.all_to_all(view, MODE, split_axis=1, concat_axis=1, tiled=True)
        current = swapped.reshape(2, width, rows)
        pick = order[step]
        matrix = lax.dynamic_index_in_dim(everything, pick, 0, keepdims=False)
        local = absorb(matrix, current).astype(jnp.bfloat16)
    offset = lax.axis_index(MODE) * rows
    column_local = column_bits - offset
    inside = jnp.logical_and(column_local >= 0, column_local < rows)
    flat_index = row_bits * rows + jnp.clip(column_local, 0, rows - 1)
    flat = local.reshape(2, width * rows)
    values = jnp.take(flat, flat_index, axis=1).astype(jnp.float32)
    values = jnp.where(inside[None, :], values, jnp.zeros_like(values))
    total_amps = over_axes(values, CUTS_MODE)
    share = values.shape[1] // lax.axis_size(CUTS_MODE)
    amplitudes = lax.dynamic_slice_in_dim(total_amps, lax.axis_index(CUTS_MODE) * share, share, 1)
    return (local[None], amplitudes)


def solution(mesh):
    finer = Mesh(
        mesh.devices.reshape(2, 2, 4, 4, 8), ("cuts_0", "cuts_1", "mode_0", "mode_1", "mode_2")
    )
    placed = (P(CUTS, None, None, MODE), P(None, None, None, MODE), P(), P(), P(), P())
    return jax.shard_map(
        body,
        mesh=finer,
        in_specs=placed,
        out_specs=(P(CUTS, None, None, MODE), P(None, CUTS_MODE)),
        check_vma=False,
    )
```

profile of v0, /device:TPU:4, one launch (start us, length us, event | category | flops | bytes accessed | tf_op | source)
XLA Modules:
  0.0 671.8 jit_solution(10324625984427429543)
XLA Ops:
  8.1 33.4 %all-gather.2 = bf16[24,2,344,8]{2,3,1,0:T(8,128)(2,1)} all-gather(bf16[3,2,344,8]{2,3,1,0:T(8,128)(2,1)S(1)} %get-tuple-element.14), channel_id=4, replica_groups=mesh['cuts_0'=2,'cuts_1'=2,'mode_0'=4,'mode_1'=4,'mode_2'=8] {'mode_2'}, dimensions={0}, use_global_device_ids=true | all-gather | bytes 297216 | tf_op jit(solution)/shard_map/all_gather | solution.py:20
  42.4 10.8 %all-gather = bf16[12,2,336,8]{2,3,1,0:T(8,128)(2,1)S(1)} all-gather(bf16[3,2,336,8]{2,3,1,0:T(8,128)(2,1)S(1)} %split.9), channel_id=2, replica_groups=mesh['cuts_0'=2,'cuts_1'=2,'mode_0'=4,'mode_1'=4,'mode_2'=8] {'mode_0'}, dimensions={0}, use_global_device_ids=true | all-gather | bytes 161280 | tf_op jit(solution)/shard_map/all_gather | solution.py:20
  53.2 29.4 %all_gather.28 = bf16[32,3,2,336,8]{3,4,2,1,0:T(8,128)(2,1)} all-gather(bf16[4,3,2,336,8]{3,4,2,1,0:T(8,128)(2,1)S(1)} %bitcast.161), channel_id=1, replica_groups=mesh['cuts_0'=2,'cuts_1'=2,'mode_0'=4,'mode_1'=4,'mode_2'=8] {'mode_2'}, dimensions={0}, use_global_device_ids=true | all-gather | bytes 1161216 | tf_op jit(solution)/shard_map/all_gather | solution.py:20
  82.6 13.6 %all-gather.1 = bf16[12,2,344,8]{2,3,1,0:T(8,128)(2,1)S(1)} all-gather(bf16[3,2,344,8]{2,3,1,0:T(8,128)(2,1)S(1)} %get-tuple-element.13), channel_id=3, replica_groups=mesh['cuts_0'=2,'cuts_1'=2,'mode_0'=4,'mode_1'=4,'mode_2'=8] {'mode_1'}, dimensions={0}, use_global_device_ids=true | all-gather | bytes 165120 | tf_op jit(solution)/shard_map/all_gather | solution.py:20
  96.3 13.6 %all_gather.31 = bf16[16,3,2,344,8]{3,4,2,1,0:T(8,128)(2,1)} all-gather(bf16[4,3,2,344,8]{3,4,2,1,0:T(8,128)(2,1)S(1)} %bitcast.162), channel_id=1, replica_groups=mesh['cuts_0'=2,'cuts_1'=2,'mode_0'=4,'mode_1'=4,'mode_2'=8] {'mode_0'}, dimensions={0}, use_global_device_ids=true | all-gather | bytes 660480 | tf_op jit(solution)/shard_map/all_gather | solution.py:20
  121.3 11.7 %all-to-all-start = ((bf16[2,128,8,128]{3,2,0,1:T(8,128)(2,1)}), bf16[2,128,8,128]{3,2,0,1:T(8,128)(2,1)S(1)}, u32[]{:S(2)}, u32[]{:S(2)}) async-start(bf16[2,128,8,128]{3,2,0,1:T(8,128)(2,1)} %copy.45), calls=%async_computation | async-start | bytes 1048576 | tf_op jit(solution)/shard_map/all_to_all | solution.py:69
  136.4 48.8 %all-gather.8.cloned.1.call-done = bf16[128,3,2,336,8]{3,4,2,1,0:T(8,128)(2,1)} async-done(((bf16[32,3,2,336,8]{3,4,2,1,0:T(8,128)(2,1)}), bf16[128,3,2,336,8]{3,4,2,1,0:T(8,128)(2,1)}) %all-gather.8.cloned.1.call-update) | async-done | bytes 4128784 | tf_op jit(solution)/shard_map/all_gather | solution.py:20
  185.1 5.2 copy.41
  190.4 61.7 %all-gather.10.cloned.1.call-done = bf16[128,3,2,344,8]{3,4,2,1,0:T(8,128)(2,1)} async-done(((bf16[16,3,2,344,8]{3,4,2,1,0:T(8,128)(2,1)}), bf16[128,3,2,344,8]{3,4,2,1,0:T(8,128)(2,1)}) %all-gather.10.cloned.1.call-update) | async-done | bytes 4227088 | tf_op jit(solution)/shard_map/all_gather | solution.py:20
  252.0 5.2 copy.42
  257.2 51.9 %all-gather.14.cloned.1.call-done = bf16[128,3,2,344,8]{3,4,2,1,0:T(8,128)(2,1)} async-done(((bf16[32,3,2,344,8]{3,4,2,1,0:T(8,128)(2,1)}), bf16[128,3,2,344,8]{3,4,2,1,0:T(8,128)(2,1)}) %all-gather.14.cloned.1.call-update) | async-done | bytes 4227088 | tf_op jit(solution)/shard_map/all_gather | solution.py:20
  309.1 13.7 %copy_bitcast_fusion = bf16[3,2,1024,1024]{2,3,1,0:T(8,128)(2,1)} fusion(bf16[128,3,2,344,8]{3,4,2,1,0:T(8,128)(2,1)} %all-gather.14.cloned.1.call-done, bf16[128,3,2,344,8]{3,4,2,1,0:T(8,128)(2,1)} %bitcast.153, bf16[128,3,2,336,8]{3,4,2,1,0:T(8,128)(2,1)} %bitcast.152), kind=kLoop, calls=%fused_computation.5 | loop fusion | flops 37748736 | bytes 25165824 | tf_op jit(solution)/shard_map/reshape | solution.py:30
  336.4 3.7 broadcast_select_fusion.1
  341.0 14.8 %all-to-all-start.1 = ((bf16[2,128,8,128]{3,2,0,1:T(8,128)(2,1)}), bf16[2,128,8,128]{3,2,0,1:T(8,128)(2,1)S(1)}, u32[]{:S(2)}, u32[]{:S(2)}) async-start(bf16[2,128,8,128]{3,2,0,1:T(8,128)(2,1)} %copy.49), calls=%async_computation.1 | async-start | bytes 1048576 | tf_op jit(solution)/shard_map/all_to_all | solution.py:69
  357.9 15.8 %all-to-all-done.1 = bf16[2,128,8,128]{3,2,0,1:T(8,128)(2,1)S(1)} async-done(((bf16[2,128,8,128]{3,2,0,1:T(8,128)(2,1)}), bf16[2,128,8,128]{3,2,0,1:T(8,128)(2,1)S(1)}, u32[]{:S(2)}, u32[]{:S(2)}) %all-to-all-start.1) | async-done | bytes 524320 | tf_op jit(solution)/shard_map/all_to_all | solution.py:69
  391.8 8.2 %all-to-all-start.2 = ((bf16[2,128,8,128]{3,2,0,1:T(8,128)(2,1)}), bf16[2,128,8,128]{3,2,0,1:T(8,128)(2,1)S(1)}, u32[]{:S(2)}, u32[]{:S(2)}) async-start(bf16[2,128,8,128]{3,2,0,1:T(8,128)(2,1)} %copy.53), calls=%async_computation.2 | async-start | bytes 1048576 | tf_op jit(solution)/shard_map/all_to_all | solution.py:69
  401.9 15.7 %all-to-all-done.2 = bf16[2,128,8,128]{3,2,0,1:T(8,128)(2,1)S(1)} async-done(((bf16[2,128,8,128]{3,2,0,1:T(8,128)(2,1)}), bf16[2,128,8,128]{3,2,0,1:T(8,128)(2,1)S(1)}, u32[]{:S(2)}, u32[]{:S(2)}) %all-to-all-start.2) | async-done | bytes 524320 | tf_op jit(solution)/shard_map/all_to_all | solution.py:69
  429.6 20.3 %copy.56 = bf16[2,131072]{0,1:T(8,128)(2,1)} copy(bf16[2,131072]{1,0:T(2,128)(2,1)S(1)} %pad_maximum_fusion.3) | data formatting | bytes 1048576 | tf_op jit(solution)/shard_map/stack | solution.py:57
  449.8 21.6 %gather_fusion = bf16[2048,2]{1,0:T(8,128)(2,1)S(1)} fusion(bf16[2,131072]{0,1:T(8,128)(2,1)} %copy.56, s32[2048]{0:T(1024)S(1)} %broadcast_clamp_fusion), kind=kCustom, calls=%fused_computation.3 | custom fusion | bytes 24576 | tf_op jit(solution)/shard_map/jit(_take)/gather | solution.py:79
  472.2 28.2 %psum.35 = f32[2,2048]{0,1:T(8,128)S(1)} all-reduce(f32[2,2048]{0,1:T(8,128)S(1)} %select_bitcast_fusion), channel_id=1, replica_groups=mesh['cuts_0'=2,'cuts_1'=2,'mode_0'=4,'mode_1'=4,'mode_2'=8] {'cuts_0'}, use_global_device_ids=true, to_apply=%region_0.0 | all-reduce | flops 4096 | bytes 32768 | tf_op jit(solution)/shard_map/psum | solution.py:45
  500.5 5.7 psum.36
  506.1 44.0 %psum.37 = f32[2,2048]{0,1:T(8,128)S(1)} all-reduce(f32[2,2048]{0,1:T(8,128)S(1)} %psum.36), channel_id=1, replica_groups=mesh['cuts_0'=2,'cuts_1'=2,'mode_0'=4,'mode_1'=4,'mode_2'=8] {'mode_0'}, use_global_device_ids=true, to_apply=%region_2.4 | all-reduce | flops 4096 | bytes 32768 | tf_op jit(solution)/shard_map/psum | solution.py:45
  550.2 53.7 %psum.38 = f32[2,2048]{0,1:T(8,128)S(1)} all-reduce(f32[2,2048]{0,1:T(8,128)S(1)} %psum.37), channel_id=1, replica_groups=mesh['cuts_0'=2,'cuts_1'=2,'mode_0'=4,'mode_1'=4,'mode_2'=8] {'mode_1'}, use_global_device_ids=true, to_apply=%region_3.5 | all-reduce | flops 4096 | bytes 32768 | tf_op jit(solution)/shard_map/psum | solution.py:45
  603.9 60.6 %psum.39 = f32[2,2048]{0,1:T(8,128)S(1)} all-reduce(f32[2,2048]{0,1:T(8,128)S(1)} %psum.38), channel_id=1, replica_groups=mesh['cuts_0'=2,'cuts_1'=2,'mode_0'=4,'mode_1'=4,'mode_2'=8] {'mode_2'}, use_global_device_ids=true, to_apply=%region_4.6 | all-reduce | flops 4096 | bytes 32768 | tf_op jit(solution)/shard_map/psum | solution.py:45
  (57 shorter events, 60.5 us)
Async XLA Ops:
  7.2 102.8 %all-gather.12.cloned.1.call-start = ((), (), s32[]{:S(2)}) async-start(), calls=%async_computation.5 | async-start | bytes 1474560 | tf_op jit(solution)/shard_map/all_gather | solution.py:20
  41.6 143.6 %all-gather.8.cloned.1.call-start = ((), (), s32[]{:S(2)}) async-start(), calls=%async_computation.3 | async-start | bytes 5898240 | tf_op jit(solution)/shard_map/all_gather | solution.py:20
  82.6 169.5 %all-gather.10.cloned.1.call-start = ((), (), s32[]{:S(2)}) async-start(), calls=%async_computation.4 | async-start | bytes 5308416 | tf_op jit(solution)/shard_map/all_gather | solution.py:20
  109.9 199.2 %all-gather.14.cloned.1.call-start = ((), (), s32[]{:S(2)}) async-start(), calls=%async_computation.6 | async-start | bytes 5898240 | tf_op jit(solution)/shard_map/all_gather | solution.py:20
  121.3 201.6 %all-to-all-start = ((bf16[2,128,8,128]{3,2,0,1:T(8,128)(2,1)}), bf16[2,128,8,128]{3,2,0,1:T(8,128)(2,1)S(1)}, u32[]{:S(2)}, u32[]{:S(2)}) async-start(bf16[2,128,8,128]{3,2,0,1:T(8,128)(2,1)} %copy.45), calls=%async_computation | async-start | bytes 1048576 | tf_op jit(solution)/shard_map/all_to_all | solution.py:69
  332.1 69.7 %copy-start = (s32[2048]{0:T(1024)S(1)}, s32[2048]{0:T(1024)}, u32[]{:S(2)}) copy-start(s32[2048]{0:T(1024)} %param.13) | copy-start | bytes 24580
  332.1 69.7 %copy-start.1 = (s32[2048]{0:T(1024)S(1)}, s32[2048]{0:T(1024)}, u32[]{:S(2)}) copy-start(s32[2048]{0:T(1024)} %param.12) | copy-start | bytes 24580
  341.0 32.6 %all-to-all-start.1 = ((bf16[2,128,8,128]{3,2,0,1:T(8,128)(2,1)}), bf16[2,128,8,128]{3,2,0,1:T(8,128)(2,1)S(1)}, u32[]{:S(2)}, u32[]{:S(2)}) async-start(bf16[2,128,8,128]{3,2,0,1:T(8,128)(2,1)} %copy.49), calls=%async_computation.1 | async-start | bytes 1048576 | tf_op jit(solution)/shard_map/all_to_all | solution.py:69
  391.8 25.8 %all-to-all-start.2 = ((bf16[2,128,8,128]{3,2,0,1:T(8,128)(2,1)}), bf16[2,128,8,128]{3,2,0,1:T(8,128)(2,1)S(1)}, u32[]{:S(2)}, u32[]{:S(2)}) async-start(bf16[2,128,8,128]{3,2,0,1:T(8,128)(2,1)} %copy.53), calls=%async_computation.2 | async-start | bytes 1048576 | tf_op jit(solution)/shard_map/all_to_all | solution.py:69
Sparse Core Ops, SparseCore 0:
  41.7 36.6 all-gather.11
  82.7 102.4 all-gather.7
  187.2 64.7 all-gather.9
  254.0 55.1 all-gather.13
where the time goes:
time: 673 us; the launch traced here: 672 us
  blocking collectives  293 us (44%)
  waiting for transfers between devices  194 us (29%)
  local copies, waits for them, and re-layouts  74.1 us (11%)
  starting transfers between devices  34.8 us (5%)
  other arithmetic  27.9 us (4%)
  matrix products  27.6 us (4%)
  between operations  19.9 us (3%)
    psum x5, blocking collectives, over_axes(): shard = lax.psum(shard, axis)  192 us
    all_gather x4, waiting for transfers between devices, gather_in_order(): blocks = lax.all_gather(blocks, axes[k], axis=0, tiled=True)  162 us
    all_gather x5, blocking collectives, gather_in_order(): blocks = lax.all_gather(blocks, axes[k], axis=0, tiled=True)  101 us
    all_to_all x3, starting transfers between devices, body(): lax.all_to_all(view, MODE, split_axis=1, concat_axis=1, tiled=True)  34.7 us
    all_to_all x3, waiting for transfers between devices, body(): lax.all_to_all(view, MODE, split_axis=1, concat_axis=1, tiled=True)  31.4 us
    dot_general x12, matrix products, product(): lax.dot_general(left, right, numbers, preferred_element_type=jnp.float32)  27.6 us
    another operation x4, local copies, waits for them, and re-layouts, absorb(): return jnp.stack([real, imag], axis=0)  22.1 us
    gather x1, local copies, waits for them, and re-layouts, body(): values = jnp.take(flat, flat_index, axis=1).astype(jnp.float32)  21.6 us
  transfers between devices with their start and end apart: 7, of which 5 were waited for; matrix products, arithmetic and copies ran while one was open for 6% of the time, Pallas kernels for 0%

commit v1 on v0

--- a/solution.py
+++ b/solution.py
@@ -7,6 +7,7 @@
 MODE = ("mode_0", "mode_1", "mode_2")
 CUTS_MODE = ("cuts_0", "cuts_1", "mode_0", "mode_1", "mode_2")
 CUTS = ("cuts_0", "cuts_1")
+pieces_all_press = lambda sheet, mesh_name: jnp.sum(lax.all_gather(sheet, mesh_name), 0)
 
 
 def cut_rows(length, count):
@@ -42,7 +43,7 @@
 
 def over_axes(shard, axes):
     for axis in axes:
-        shard = lax.psum(shard, axis)
+        shard = pieces_all_press(shard, axis)
     return shard
 
 

time: 673 us -> 541 us (0.80)
  the two profiles are of different devices: /device:TPU:4 before, /device:TPU:8 now
where the time goes in v1:
time: 541 us; the launch traced here: 540 us
  waiting for transfers between devices  198 us (37%)
  blocking collectives  161 us (30%)
  local copies, waits for them, and re-layouts  75 us (14%)
  starting transfers between devices  30.4 us (6%)
  matrix products  27.6 us (5%)
  other arithmetic  27.3 us (5%)
  between operations  19.9 us (4%)
    all_gather x4, waiting for transfers between devices, gather_in_order(): blocks = lax.all_gather(blocks, axes[k], axis=0, tiled=True)  163 us
    all_gather x5, blocking collectives, gather_in_order(): blocks = lax.all_gather(blocks, axes[k], axis=0, tiled=True)  102 us
    all_gather x5, blocking collectives, lax.all_gather(sheet, mesh_name)  58.8 us
    all_to_all x3, waiting for transfers between devices, body(): lax.all_to_all(view, MODE, split_axis=1, concat_axis=1, tiled=True)  34.1 us
    all_to_all x3, starting transfers between devices, body(): lax.all_to_all(view, MODE, split_axis=1, concat_axis=1, tiled=True)  30.2 us
    dot_general x12, matrix products, product(): lax.dot_general(left, right, numbers, preferred_element_type=jnp.float32)  27.6 us
    another operation x4, local copies, waits for them, and re-layouts, absorb(): return jnp.stack([real, imag], axis=0)  22.1 us
    gather x2, local copies, waits for them, and re-layouts, body(): values = jnp.take(flat, flat_index, axis=1).astype(jnp.float32)  21.8 us
  transfers between devices with their start and end apart: 7, of which 5 were waited for; matrix products, arithmetic and copies ran while one was open for 7% of the time, Pallas kernels for 0%

profile of v1, /device:TPU:8, one launch (start us, length us, event | category | flops | bytes accessed | tf_op | source)
XLA Modules:
  0.0 539.5 jit_solution(5348499695694887027)
XLA Ops:
  8.1 33.4 %all-gather.2 = bf16[24,2,344,8]{2,3,1,0:T(8,128)(2,1)} all-gather(bf16[3,2,344,8]{2,3,1,0:T(8,128)(2,1)S(1)} %get-tuple-element.4), channel_id=4, replica_groups=mesh['cuts_0'=2,'cuts_1'=2,'mode_0'=4,'mode_1'=4,'mode_2'=8] {'mode_2'}, dimensions={0}, use_global_device_ids=true | all-gather | bytes 297216 | tf_op jit(solution)/shard_map/all_gather | solution.py:21
  42.4 12.4 %all-gather = bf16[12,2,336,8]{2,3,1,0:T(8,128)(2,1)S(1)} all-gather(bf16[3,2,336,8]{2,3,1,0:T(8,128)(2,1)S(1)} %split.9), channel_id=2, replica_groups=mesh['cuts_0'=2,'cuts_1'=2,'mode_0'=4,'mode_1'=4,'mode_2'=8] {'mode_0'}, dimensions={0}, use_global_device_ids=true | all-gather | bytes 161280 | tf_op jit(solution)/shard_map/all_gather | solution.py:21
  54.7 29.3 %all_gather.56 = bf16[32,3,2,336,8]{3,4,2,1,0:T(8,128)(2,1)} all-gather(bf16[4,3,2,336,8]{3,4,2,1,0:T(8,128)(2,1)S(1)} %bitcast.168), channel_id=1, replica_groups=mesh['cuts_0'=2,'cuts_1'=2,'mode_0'=4,'mode_1'=4,'mode_2'=8] {'mode_2'}, dimensions={0}, use_global_device_ids=true | all-gather | bytes 1161216 | tf_op jit(solution)/shard_map/all_gather | solution.py:21
  84.2 13.6 %all-gather.1 = bf16[12,2,344,8]{2,3,1,0:T(8,128)(2,1)S(1)} all-gather(bf16[3,2,344,8]{2,3,1,0:T(8,128)(2,1)S(1)} %get-tuple-element.3), channel_id=3, replica_groups=mesh['cuts_0'=2,'cuts_1'=2,'mode_0'=4,'mode_1'=4,'mode_2'=8] {'mode_1'}, dimensions={0}, use_global_device_ids=true | all-gather | bytes 165120 | tf_op jit(solution)/shard_map/all_gather | solution.py:21
  97.8 13.6 %all_gather.59 = bf16[16,3,2,344,8]{3,4,2,1,0:T(8,128)(2,1)} all-gather(bf16[4,3,2,344,8]{3,4,2,1,0:T(8,128)(2,1)S(1)} %bitcast.169), channel_id=1, replica_groups=mesh['cuts_0'=2,'cuts_1'=2,'mode_0'=4,'mode_1'=4,'mode_2'=8] {'mode_0'}, dimensions={0}, use_global_device_ids=true | all-gather | bytes 660480 | tf_op jit(solution)/shard_map/all_gather | solution.py:21
  122.8 9.8 %all-to-all-start = ((bf16[2,128,8,128]{3,2,0,1:T(8,128)(2,1)}), bf16[2,128,8,128]{3,2,0,1:T(8,128)(2,1)S(1)}, u32[]{:S(2)}, u32[]{:S(2)}) async-start(bf16[2,128,8,128]{3,2,0,1:T(8,128)(2,1)} %copy.62), calls=%async_computation | async-start | bytes 1048576 | tf_op jit(solution)/shard_map/all_to_all | solution.py:70
  136.0 51.9 %all-gather.16.cloned.1.call-done = bf16[128,3,2,336,8]{3,4,2,1,0:T(8,128)(2,1)} async-done(((bf16[32,3,2,336,8]{3,4,2,1,0:T(8,128)(2,1)}), bf16[128,3,2,336,8]{3,4,2,1,0:T(8,128)(2,1)}) %all-gather.16.cloned.1.call-update) | async-done | bytes 4128784 | tf_op jit(solution)/shard_map/all_gather | solution.py:21
  187.9 5.2 copy.58
  193.1 58.9 %all-gather.18.cloned.1.call-done = bf16[128,3,2,344,8]{3,4,2,1,0:T(8,128)(2,1)} async-done(((bf16[16,3,2,344,8]{3,4,2,1,0:T(8,128)(2,1)}), bf16[128,3,2,344,8]{3,4,2,1,0:T(8,128)(2,1)}) %all-gather.18.cloned.1.call-update) | async-done | bytes 4227088 | tf_op jit(solution)/shard_map/all_gather | solution.py:21
  252.0 5.2 copy.59
  257.2 52.7 %all-gather.22.cloned.1.call-done = bf16[128,3,2,344,8]{3,4,2,1,0:T(8,128)(2,1)} async-done(((bf16[32,3,2,344,8]{3,4,2,1,0:T(8,128)(2,1)}), bf16[128,3,2,344,8]{3,4,2,1,0:T(8,128)(2,1)}) %all-gather.22.cloned.1.call-update) | async-done | bytes 4227088 | tf_op jit(solution)/shard_map/all_gather | solution.py:21
  309.9 13.7 %copy_bitcast_fusion = bf16[3,2,1024,1024]{2,3,1,0:T(8,128)(2,1)} fusion(bf16[128,3,2,344,8]{3,4,2,1,0:T(8,128)(2,1)} %all-gather.22.cloned.1.call-done, bf16[128,3,2,344,8]{3,4,2,1,0:T(8,128)(2,1)} %bitcast.159, bf16[128,3,2,336,8]{3,4,2,1,0:T(8,128)(2,1)} %bitcast.158), kind=kLoop, calls=%fused_computation.5 | loop fusion | flops 37748736 | bytes 25165824 | tf_op jit(solution)/shard_map/reshape | solution.py:31
  337.2 3.7 broadcast_select_fusion.1
  341.8 13.6 %all-to-all-start.1 = ((bf16[2,128,8,128]{3,2,0,1:T(8,128)(2,1)}), bf16[2,128,8,128]{3,2,0,1:T(8,128)(2,1)S(1)}, u32[]{:S(2)}, u32[]{:S(2)}) async-start(bf16[2,128,8,128]{3,2,0,1:T(8,128)(2,1)} %copy.66), calls=%async_computation.1 | async-start | bytes 1048576 | tf_op jit(solution)/shard_map/all_to_all | solution.py:70
  357.5 17.1 %all-to-all-done.1 = bf16[2,128,8,128]{3,2,0,1:T(8,128)(2,1)S(1)} async-done(((bf16[2,128,8,128]{3,2,0,1:T(8,128)(2,1)}), bf16[2,128,8,128]{3,2,0,1:T(8,128)(2,1)S(1)}, u32[]{:S(2)}, u32[]{:S(2)}) %all-to-all-start.1) | async-done | bytes 524320 | tf_op jit(solution)/shard_map/all_to_all | solution.py:70
  388.1 3.7 broadcast_select_fusion
  392.7 6.8 %all-to-all-start.2 = ((bf16[2,128,8,128]{3,2,0,1:T(8,128)(2,1)}), bf16[2,128,8,128]{3,2,0,1:T(8,128)(2,1)S(1)}, u32[]{:S(2)}, u32[]{:S(2)}) async-start(bf16[2,128,8,128]{3,2,0,1:T(8,128)(2,1)} %copy.70), calls=%async_computation.2 | async-start | bytes 1048576 | tf_op jit(solution)/shard_map/all_to_all | solution.py:70
  401.5 17.0 %all-to-all-done.2 = bf16[2,128,8,128]{3,2,0,1:T(8,128)(2,1)S(1)} async-done(((bf16[2,128,8,128]{3,2,0,1:T(8,128)(2,1)}), bf16[2,128,8,128]{3,2,0,1:T(8,128)(2,1)S(1)}, u32[]{:S(2)}, u32[]{:S(2)}) %all-to-all-start.2) | async-done | bytes 524320 | tf_op jit(solution)/shard_map/all_to_all | solution.py:70
  430.6 20.3 %copy.73 = bf16[2,131072]{0,1:T(8,128)(2,1)} copy(bf16[2,131072]{1,0:T(2,128)(2,1)S(1)} %pad_maximum_fusion.3) | data formatting | bytes 1048576 | tf_op jit(solution)/shard_map/stack | solution.py:58
  450.8 21.6 %gather_fusion = bf16[2048,2]{1,0:T(8,128)(2,1)S(1)} fusion(bf16[2,131072]{0,1:T(8,128)(2,1)} %copy.73, s32[2048]{0:T(1024)S(1)} %broadcast_clamp_fusion), kind=kCustom, calls=%fused_computation.3 | custom fusion | bytes 24576 | tf_op jit(solution)/shard_map/jit(_take)/gather | solution.py:80
  472.7 8.3 %all_gather.64 = f32[2,2,2048]{2,1,0:T(2,128)S(1)} all-gather(f32[1,2,2048]{2,1,0:T(2,128)S(1)} %convert_select_fusion), channel_id=1, replica_groups=mesh['cuts_0'=2,'cuts_1'=2,'mode_0'=4,'mode_1'=4,'mode_2'=8] {'cuts_0'}, dimensions={0}, use_global_device_ids=true | all-gather | bytes 49152 | tf_op jit(solution)/shard_map/all_gather | solution.py:10
  483.6 11.9 %all-gather.8 = f32[4,2,2048]{2,1,0:T(2,128)S(1)} all-gather(f32[1,2,2048]{2,1,0:T(2,128)S(1)} %bitcast.170), channel_id=6, replica_groups=mesh['cuts_0'=2,'cuts_1'=2,'mode_0'=4,'mode_1'=4,'mode_2'=8] {'mode_0'}, dimensions={0}, use_global_device_ids=true | all-gather | bytes 81920 | tf_op jit(solution)/shard_map/all_gather | solution.py:10
  495.5 12.2 %all-gather.9 = f32[4,2,2048]{2,1,0:T(2,128)S(1)} all-gather(f32[1,2,2048]{2,1,0:T(2,128)S(1)} %bitcast.171), channel_id=7, replica_groups=mesh['cuts_0'=2,'cuts_1'=2,'mode_0'=4,'mode_1'=4,'mode_2'=8] {'mode_1'}, dimensions={0}, use_global_device_ids=true | all-gather | bytes 81920 | tf_op jit(solution)/shard_map/all_gather | solution.py:10
  507.7 24.6 %all-gather.10 = f32[8,2,2048]{2,1,0:T(2,128)S(1)} all-gather(f32[1,2,2048]{2,1,0:T(2,128)S(1)} %bitcast.172), channel_id=8, replica_groups=mesh['cuts_0'=2,'cuts_1'=2,'mode_0'=4,'mode_1'=4,'mode_2'=8] {'mode_2'}, dimensions={0}, use_global_device_ids=true | all-gather | bytes 147456 | tf_op jit(solution)/shard_map/all_gather | solution.py:10
  (64 shorter events, 59.0 us)
Async XLA Ops:
  7.2 104.4 %all-gather.20.cloned.1.call-start = ((), (), s32[]{:S(2)}) async-start(), calls=%async_computation.5 | async-start | bytes 1474560 | tf_op jit(solution)/shard_map/all_gather | solution.py:21
  41.6 146.4 %all-gather.16.cloned.1.call-start = ((), (), s32[]{:S(2)}) async-start(), calls=%async_computation.3 | async-start | bytes 5898240 | tf_op jit(solution)/shard_map/all_gather | solution.py:21
  84.1 167.9 %all-gather.18.cloned.1.call-start = ((), (), s32[]{:S(2)}) async-start(), calls=%async_computation.4 | async-start | bytes 5308416 | tf_op jit(solution)/shard_map/all_gather | solution.py:21
  111.4 198.5 %all-gather.22.cloned.1.call-start = ((), (), s32[]{:S(2)}) async-start(), calls=%async_computation.6 | async-start | bytes 5898240 | tf_op jit(solution)/shard_map/all_gather | solution.py:21
  122.8 200.9 %all-to-all-start = ((bf16[2,128,8,128]{3,2,0,1:T(8,128)(2,1)}), bf16[2,128,8,128]{3,2,0,1:T(8,128)(2,1)S(1)}, u32[]{:S(2)}, u32[]{:S(2)}) async-start(bf16[2,128,8,128]{3,2,0,1:T(8,128)(2,1)} %copy.62), calls=%async_computation | async-start | bytes 1048576 | tf_op jit(solution)/shard_map/all_to_all | solution.py:70
  332.9 68.6 %copy-start = (s32[2048]{0:T(1024)S(1)}, s32[2048]{0:T(1024)}, u32[]{:S(2)}) copy-start(s32[2048]{0:T(1024)} %param.13) | copy-start | bytes 24580
  332.9 68.6 %copy-start.1 = (s32[2048]{0:T(1024)S(1)}, s32[2048]{0:T(1024)}, u32[]{:S(2)}) copy-start(s32[2048]{0:T(1024)} %param.12) | copy-start | bytes 24580
  341.8 32.8 %all-to-all-start.1 = ((bf16[2,128,8,128]{3,2,0,1:T(8,128)(2,1)}), bf16[2,128,8,128]{3,2,0,1:T(8,128)(2,1)S(1)}, u32[]{:S(2)}, u32[]{:S(2)}) async-start(bf16[2,128,8,128]{3,2,0,1:T(8,128)(2,1)} %copy.66), calls=%async_computation.1 | async-start | bytes 1048576 | tf_op jit(solution)/shard_map/all_to_all | solution.py:70
  392.7 25.8 %all-to-all-start.2 = ((bf16[2,128,8,128]{3,2,0,1:T(8,128)(2,1)}), bf16[2,128,8,128]{3,2,0,1:T(8,128)(2,1)S(1)}, u32[]{:S(2)}, u32[]{:S(2)}) async-start(bf16[2,128,8,128]{3,2,0,1:T(8,128)(2,1)} %copy.70), calls=%async_computation.2 | async-start | bytes 1048576 | tf_op jit(solution)/shard_map/all_to_all | solution.py:70
Sparse Core Ops, SparseCore 0:
  41.7 35.2 all-gather.19
  84.2 103.6 all-gather.15
  190.0 61.9 all-gather.17
  253.9 55.9 all-gather.21
